TPU v7x, 32 devices: a whole 2x2x4 slice. The times are simulated.
32 devices in a mesh: cen: 8 (over y, x, core), grp: 4 (over z).
Axes of the slice: x: 2, y: 2, z: 4, core: 2. Of those that a mesh axis runs over, the one named last changes fastest.
Arguments:
- centers: bfloat16 [65536, 1024], P(('cen', 'grp')), may hold values from -2 to 2
- coefficients: float32 [65536, 256], P(('cen', 'grp')), may hold values from -0.09375 to 0.09375
- batch_index: int32 [256], P(('cen', 'grp')), may hold values from 0 to 65535, as said below
- batch_labels: float32 [256, 256], P(('cen', 'grp')), may hold values from -24 to 24
- nystrom_index: int32 [16384], P(('cen', 'grp')), may hold values from 0 to 65535, as said below
- eigenvectors: float32 [16384, 512], P(('cen', 'grp')), may hold values from -0.046875 to 0.046875
- eigen_weights: float32 [512], replicated, may hold values from 0.002 to 0.05
Outputs:
- residual: float32 [256, 256], P(('cen', 'grp'))
- correction: float32 [16384, 256], P(('cen', 'grp'))
Inputs may be any that keep to these rules, and one draw needn't show every extreme that they name: `batch_index`: for each j, entries 8 * j to 8 * j + 7 are distinct rows among j * 2048 to j * 2048 + 2047. `nystrom_index`: for each j, entries 512 * j to 512 * j + 511 are distinct rows among j * 2048 to j * 2048 + 2047.
All inputs are finite; a program needn't handle non-finite values.
Results may differ from a plain program's by a relative error of at most 0.0003.
Values may be sent and summed in bfloat16 or wider, within the bound.
No kernel may reach another device: no remote copies, remote signals or barrier semaphores. Data moves between devices by JAX's collectives and lax.ppermute only.
A program may use at most 64 MiB of HBM per device.

v0:
```python
import jax
import jax.numpy as jnp
from jax import lax
from jax.sharding import PartitionSpec as P


def inner_kernel(left, right):
    scores = lax.dot_general(
        left, right, (((1,), (1,)), ((), ())), preferred_element_type=jnp.float32
    )
    return jnp.exp(scores / 32.0)


def exact_dot(left, right):
    return jnp.dot(left, right, precision=lax.Precision.HIGHEST, preferred_element_type=jnp.float32)


def body(
    centers, coefficients, batch_index, batch_labels, nystrom_index, eigenvectors, eigen_weights
):
    center_count = centers.shape[0]
    owned_rows = jnp.take(centers, batch_index % center_count, axis=0)
    batch_x = lax.all_gather(owned_rows, ("cen", "grp"), axis=0, tiled=True)
    partial_pred = exact_dot(inner_kernel(batch_x, centers), coefficients)
    nystrom_x = jnp.take(centers, nystrom_index % center_count, axis=0)
    nystrom_kernel = inner_kernel(nystrom_x, batch_x)
    batch_rows = batch_labels.shape[0]
    first_row = lax.axis_index(("cen", "grp")) * batch_rows
    own_part = lax.dynamic_slice_in_dim(partial_pred, first_row, batch_rows, 0) - batch_labels
    summand = lax.dynamic_update_slice_in_dim(partial_pred, own_part, first_row, 0)
    residual_all = lax.psum(summand, ("cen", "grp"))
    own_residual = lax.dynamic_slice_in_dim(residual_all, first_row, batch_rows, 0)
    local_products = exact_dot(nystrom_kernel, residual_all)
    projected = lax.psum(exact_dot(eigenvectors.T, local_products), ("cen", "grp"))
    correction = exact_dot(eigenvectors, eigen_weights[:, None] * projected)
    return (own_residual, correction)


def solution(mesh):
    in_specs = (
        P(("cen", "grp"), None),
        P(("cen", "grp"), None),
        P(("cen", "grp")),
        P(("cen", "grp"), None),
        P(("cen", "grp")),
        P(("cen", "grp"), None),
        P(),
    )
    out_specs = (P(("cen", "grp"), None), P(("cen", "grp"), None))
    return jax.shard_map(body, mesh=mesh, in_specs=in_specs, out_specs=out_specs, check_vma=False)
```

profile of v0, /device:TPU:0, one launch (start us, length us, event | category | flops | bytes accessed | tf_op | source)
XLA Modules:
  0.0 365.1 jit_solution(11219667917849283521)
XLA Ops:
  7.2 0.0 copy-start
  7.2 0.0 all-reduce.3.cloned.1.call-start
  7.2 0.8 compare_and_fusion.1
  8.0 3.3 gather_fusion
  11.4 0.1 broadcast_select_fusion
  11.4 73.9 %all_gather.3 = bf16[256,1024]{1,0:T(8,128)(2,1)S(1)} all-gather(bf16[8,1024]{1,0:T(8,128)(2,1)S(1)} %broadcast_select_fusion), channel_id=1, replica_groups=mesh['cen'=8,'grp'=4] {'cen','grp'}, dimensions={0}, use_global_device_ids=true | all-gather | bytes 540672 | tf_op jit(solution)/shard_map/all_gather | solution.py:23
  85.4 0.0 copy-start.3
  85.4 0.8 copy-done.3
  86.2 4.9 %fusion = f32[256,2048]{1,0:T(8,128)} fusion(bf16[256,1024]{1,0:T(8,128)(2,1)S(1)} %all_gather.3, bf16[2048,1024]{1,0:T(8,128)(2,1)} %param.7), kind=kOutput, calls=%fused_computation.3 | convolution fusion | flops 1074266112 | bytes 6815744 | tf_op jit(solution)/shard_map/dot_general | solution.py:8
  91.1 0.0 copy-done
  91.1 0.0 copy-start.4
  91.1 0.0 copy-start.6
  91.1 3.5 fusion.10
  94.6 0.0 copy-done.4
  94.6 0.0 copy-start.2
  94.6 0.7 copy-done.2
  95.3 0.0 all-reduce.3.cloned.1.call-update
  95.4 0.0 all-reduce.5.cloned.1.call-start
  95.4 0.0 copy-done.6
  95.5 6.2 %gather_fusion.1 = bf16[512,1024]{1,0:T(8,128)(2,1)} fusion(bf16[2048,1024]{1,0:T(8,128)(2,1)} %param.7, s32[1024]{0:T(1024)S(1)} %pad_clamp_fusion), kind=kCustom, calls=%fused_computation.1 | custom fusion | bytes 2099200 | tf_op jit(solution)/shard_map/jit(_take)/gather | solution.py:25
  101.7 0.0 copy-start.1
  101.7 2.8 fusion.1
  104.4 0.0 copy-start.5
  104.4 114.0 %all-reduce.3.cloned.1.call-done = f32[256,256]{1,0:T(8,128)} async-done(((f32[256,256]{1,0:T(8,128)}), f32[256,256]{1,0:T(8,128)}) %all-reduce.3.cloned.1.call-update) | async-done | bytes 262160 | tf_op jit(solution)/shard_map/psum | solution.py:31
  218.5 1.7 fusion.11
  220.2 0.0 copy-done.1
  220.2 2.6 convolution_bitcast_fusion.1
  222.8 0.0 all-reduce.5.cloned.1.call-update
  222.8 1.3 constant_dynamic-slice_fusion
  224.1 128.4 %all-reduce.5.cloned.1.call-done = f32[512,256]{1,0:T(8,128)} async-done(((f32[512,256]{1,0:T(8,128)}), f32[512,256]{1,0:T(8,128)}) %all-reduce.5.cloned.1.call-update) | async-done | bytes 524304 | tf_op jit(solution)/shard_map/psum | solution.py:34
  352.5 0.0 copy-done.5
  352.5 3.8 %convolution_bitcast_fusion = f32[512,256]{0,1:T(8,128)} fusion(f32[512,512]{1,0:T(8,128)S(1)} %copy-done.1, f32[512,256]{1,0:T(8,128)} %all-reduce.5.cloned.1.call-done, f32[512]{0:T(512)S(1)} %copy-done.5), kind=kOutput, calls=%fused_computation.6 | convolution fusion | flops 805437440 | bytes 2099200 | tf_op jit(solution)/shard_map/dot_general | solution.py:15
  356.2 2.0 copy.9
  (4 shorter events, 0.0 us)
Async XLA Ops:
  7.2 83.9 %copy-start = (f32[2048,256]{1,0:T(8,128)S(1)}, f32[2048,256]{1,0:T(8,128)}, u32[]{:S(2)}) copy-start(f32[2048,256]{1,0:T(8,128)} %param.8) | copy-start | bytes 6291460
  7.2 211.3 %all-reduce.3.cloned.1.call-start = ((), (), s32[]{:S(2)}) async-start(), calls=%async_computation | async-start | bytes 524288 | tf_op jit(solution)/shard_map/psum | solution.py:31
  85.4 0.8 copy-start.3
  91.1 3.5 copy-start.4
  91.1 4.3 %copy-start.6 = (s32[512]{0:T(512)S(1)}, s32[512]{0:T(512)}, u32[]{:S(2)}) copy-start(s32[512]{0:T(512)} %param.11) | copy-start | bytes 6148
  94.6 0.7 copy-start.2
  95.4 257.1 %all-reduce.5.cloned.1.call-start = ((), (), s32[]{:S(2)}) async-start(), calls=%async_computation.1 | async-start | bytes 1048576 | tf_op jit(solution)/shard_map/psum | solution.py:34
  101.7 118.5 %copy-start.1 = (f32[512,512]{1,0:T(8,128)S(1)}, f32[512,512]{1,0:T(8,128)}, u32[]{:S(2)}) copy-start(f32[512,512]{1,0:T(8,128)} %param.12) | copy-start | bytes 3145732
  104.4 248.0 %copy-start.5 = (f32[512]{0:T(512)S(1)}, f32[512]{0:T(512)}, u32[]{:S(2)}) copy-start(f32[512]{0:T(512)} %param.13) | copy-start | bytes 6148
Sparse Core Ops, SparseCore 0:
  95.5 122.9 all-reduce.2
  224.3 128.1 all-reduce.4
where the time goes:
time: 366 us; the launch traced here: 365 us
  waiting for transfers between devices  242 us (66%)
  blocking collectives  73.9 us (20%)
  matrix products  19.3 us (5%)
  local copies, waits for them, and re-layouts  14.4 us (4%)
  between operations  14.1 us (4%)
    psum x1, waiting for transfers between devices, body(): lax.psum(exact_dot(eigenvectors.T, local_products), ('cen', 'grp'))  128 us
    psum x1, waiting for transfers between devices, body(): residual_all = lax.psum(summand, ('cen', 'grp'))  114 us
    all_gather x1, blocking collectives, body(): batch_x = lax.all_gather(owned_rows, ('cen', 'grp'), axis=0, tiled=True)  73.9 us
    dot_general x4, matrix products, exact_dot(): jnp.dot(left, right, precision=lax.Precision.HIGHEST, preferred_element_t...  11.6 us
    dot_general x2, matrix products, inner_kernel(): lax.dot_general(left, right, (((1,), (1,)), ((), ())), preferred_element_...  7.7 us
  transfers between devices with their start and end apart: 2, of which 2 were waited for; matrix products, arithmetic and copies ran while one was open for 3% of the time, Pallas kernels for 0%

commit v1 on v0

--- a/solution.py
+++ b/solution.py
@@ -31,7 +31,7 @@
     residual_all = lax.psum(summand, ("cen", "grp"))
     own_residual = lax.dynamic_slice_in_dim(residual_all, first_row, batch_rows, 0)
     local_products = exact_dot(nystrom_kernel, residual_all)
-    projected = lax.psum(exact_dot(eigenvectors.T, local_products), ("cen", "grp"))
+    projected = lax.psum(lax.psum(exact_dot(eigenvectors.T, local_products), "cen"), "grp")
     correction = exact_dot(eigenvectors, eigen_weights[:, None] * projected)
     return (own_residual, correction)
 

time: 366 us -> 330 us (0.902)
  waiting for transfers between devices: 242 us -> 207 us
    psum x1 -> x2, waiting for transfers between devices: 128 us -> 92.9 us  [the longest x1 54 us: body(): lax.psum(exact_dot(eigenvectors.T, local_products), 'cen')]
  transfers between devices with their start and end apart: 2 -> 3, of which waited for: 2 -> 3; matrix products, arithmetic and copies ran while one was open for 3% -> 3% of each run, Pallas kernels for 0% -> 0%
where the time goes in v1:
time: 330 us; the launch traced here: 329 us
  waiting for transfers between devices  207 us (63%)
  blocking collectives  73.9 us (22%)
  matrix products  19.3 us (6%)
  local copies, waits for them, and re-layouts  14.4 us (4%)
  between operations  13.8 us (4%)
    psum x1, waiting for transfers between devices, body(): residual_all = lax.psum(summand, ('cen', 'grp'))  114 us
    all_gather x1, blocking collectives, body(): batch_x = lax.all_gather(owned_rows, ('cen', 'grp'), axis=0, tiled=True)  73.9 us
    psum x1, waiting for transfers between devices, body(): lax.psum(exact_dot(eigenvectors.T, local_products), 'cen')  54 us
    psum x1, waiting for transfers between devices, body(): lax.psum(lax.psum(exact_dot(eigenvectors.T, local_products), 'cen'), 'grp')  38.9 us
    dot_general x4, matrix products, exact_dot(): jnp.dot(left, right, precision=lax.Precision.HIGHEST, preferred_element_t...  11.6 us
    dot_general x2, matrix products, inner_kernel(): lax.dot_general(left, right, (((1,), (1,)), ((), ())), preferred_element_...  7.7 us
  transfers between devices with their start and end apart: 3, of which 3 were waited for; matrix products, arithmetic and copies ran while one was open for 3% of the time, Pallas kernels for 0%

profile of v1, /device:TPU:0, one launch (start us, length us, event | category | flops | bytes accessed | tf_op | source)
XLA Modules:
  0.0 329.4 jit_solution(7713597480619726172)
XLA Ops:
  7.2 0.0 copy-start
  7.2 0.0 all-reduce.4.cloned.1.call-start
  7.2 0.8 compare_and_fusion.1
  8.0 3.3 %gather_fusion = bf16[8,1024]{1,0:T(8,128)(2,1)S(1)} fusion(bf16[2048,1024]{1,0:T(8,128)(2,1)} %param.7, s32[1024]{0:T(1024)S(1)} %pad_clamp_fusion.1), kind=kCustom, calls=%fused_computation | custom fusion | bytes 32800 | tf_op jit(solution)/shard_map/jit(_take)/gather | solution.py:22
  11.4 0.1 broadcast_select_fusion
  11.4 73.9 %all_gather.3 = bf16[256,1024]{1,0:T(8,128)(2,1)S(1)} all-gather(bf16[8,1024]{1,0:T(8,128)(2,1)S(1)} %broadcast_select_fusion), channel_id=1, replica_groups=mesh['cen'=8,'grp'=4] {'cen','grp'}, dimensions={0}, use_global_device_ids=true | all-gather | bytes 540672 | tf_op jit(solution)/shard_map/all_gather | solution.py:23
  85.4 0.0 copy-start.3
  85.4 0.8 copy-done.3
  86.2 4.9 %fusion = f32[256,2048]{1,0:T(8,128)} fusion(bf16[256,1024]{1,0:T(8,128)(2,1)S(1)} %all_gather.3, bf16[2048,1024]{1,0:T(8,128)(2,1)} %param.7), kind=kOutput, calls=%fused_computation.3 | convolution fusion | flops 1074266112 | bytes 6815744 | tf_op jit(solution)/shard_map/dot_general | solution.py:8
  91.1 0.0 copy-done
  91.1 0.0 copy-start.4
  91.1 0.0 copy-start.6
  91.1 3.5 %fusion.10 = f32[256,256]{1,0:T(8,128)S(1)} fusion(f32[256,2048]{1,0:T(8,128)} %fusion, f32[2048,256]{1,0:T(8,128)S(1)} %copy-done), kind=kOutput, calls=%fused_computation.31 | convolution fusion | flops 1610612736 | bytes 4456448 | tf_op jit(solution)/shard_map/dot_general | solution.py:15
  94.6 0.0 copy-done.4
  94.6 0.0 copy-start.2
  94.6 0.7 copy-done.2
  95.3 0.0 all-reduce.4.cloned.1.call-update
  95.4 0.0 all-reduce.6.cloned.1.call-start
  95.4 0.0 copy-done.6
  95.5 6.2 %gather_fusion.1 = bf16[512,1024]{1,0:T(8,128)(2,1)} fusion(bf16[2048,1024]{1,0:T(8,128)(2,1)} %param.7, s32[1024]{0:T(1024)S(1)} %pad_clamp_fusion), kind=kCustom, calls=%fused_computation.1 | custom fusion | bytes 2099200 | tf_op jit(solution)/shard_map/jit(_take)/gather | solution.py:25
  101.7 0.0 copy-start.1
  101.7 2.8 fusion.1
  104.4 0.0 copy-start.5
  104.4 114.0 %all-reduce.4.cloned.1.call-done = f32[256,256]{1,0:T(8,128)} async-done(((f32[256,256]{1,0:T(8,128)}), f32[256,256]{1,0:T(8,128)}) %all-reduce.4.cloned.1.call-update) | async-done | bytes 262160 | tf_op jit(solution)/shard_map/psum | solution.py:31
  218.5 1.7 fusion.11
  220.2 0.0 copy-done.1
  220.2 2.6 convolution_bitcast_fusion.1
  222.8 0.0 all-reduce.6.cloned.1.call-update
  222.8 0.0 all-reduce.8.cloned.1.call-start
  222.9 54.0 %all-reduce.6.cloned.1.call-done = f32[512,256]{1,0:T(8,128)} async-done(((f32[512,256]{1,0:T(8,128)}), f32[512,256]{1,0:T(8,128)}) %all-reduce.6.cloned.1.call-update) | async-done | bytes 524304 | tf_op jit(solution)/shard_map/psum | solution.py:34
  276.8 0.0 all-reduce.8.cloned.1.call-update
  276.9 1.3 constant_dynamic-slice_fusion
  278.2 38.9 %all-reduce.8.cloned.1.call-done = f32[512,256]{1,0:T(8,128)} async-done(((f32[512,256]{1,0:T(8,128)}), f32[512,256]{1,0:T(8,128)}) %all-reduce.8.cloned.1.call-update) | async-done | bytes 524304 | tf_op jit(solution)/shard_map/psum | solution.py:34
  317.0 0.0 copy-done.5
  317.0 3.8 %convolution_bitcast_fusion = f32[512,256]{0,1:T(8,128)} fusion(f32[512,512]{1,0:T(8,128)S(1)} %copy-done.1, f32[512,256]{1,0:T(8,128)} %all-reduce.8.cloned.1.call-done, f32[512]{0:T(512)S(1)} %copy-done.5), kind=kOutput, calls=%fused_computation.6 | convolution fusion | flops 805437440 | bytes 2099200 | tf_op jit(solution)/shard_map/dot_general | solution.py:15
  320.8 2.0 copy.9
  (4 shorter events, 0.0 us)
Async XLA Ops:
  7.2 83.9 %copy-start = (f32[2048,256]{1,0:T(8,128)S(1)}, f32[2048,256]{1,0:T(8,128)}, u32[]{:S(2)}) copy-start(f32[2048,256]{1,0:T(8,128)} %param.8) | copy-start | bytes 6291460
  7.2 211.3 %all-reduce.4.cloned.1.call-start = ((), (), s32[]{:S(2)}) async-start(), calls=%async_computation | async-start | bytes 524288 | tf_op jit(solution)/shard_map/psum | solution.py:31
  85.4 0.8 copy-start.3
  91.1 3.5 %copy-start.4 = (f32[8,256]{1,0:T(8,128)S(1)}, f32[8,256]{1,0:T(8,128)}, u32[]{:S(2)}) copy-start(f32[8,256]{1,0:T(8,128)} %param.10) | copy-start | bytes 24580
  91.1 4.3 %copy-start.6 = (s32[512]{0:T(512)S(1)}, s32[512]{0:T(512)}, u32[]{:S(2)}) copy-start(s32[512]{0:T(512)} %param.11) | copy-start | bytes 6148
  94.6 0.7 copy-start.2
  95.4 181.5 %all-reduce.6.cloned.1.call-start = ((), (), s32[]{:S(2)}) async-start(), calls=%async_computation.1 | async-start | bytes 1048576 | tf_op jit(solution)/shard_map/psum | solution.py:34
  101.7 118.5 %copy-start.1 = (f32[512,512]{1,0:T(8,128)S(1)}, f32[512,512]{1,0:T(8,128)}, u32[]{:S(2)}) copy-start(f32[512,512]{1,0:T(8,128)} %param.12) | copy-start | bytes 3145732
  104.4 212.6 %copy-start.5 = (f32[512]{0:T(512)S(1)}, f32[512]{0:T(512)}, u32[]{:S(2)}) copy-start(f32[512]{0:T(512)} %param.13) | copy-start | bytes 6148
  222.8 94.2 %all-reduce.8.cloned.1.call-start = ((), (), s32[]{:S(2)}) async-start(), calls=%async_computation.2 | async-start | bytes 1048576 | tf_op jit(solution)/shard_map/psum | solution.py:34
Sparse Core Ops, SparseCore 0:
  95.5 122.9 all-reduce.3
  222.9 53.8 all-reduce.5
  279.2 37.8 all-reduce.7
